TPU v7x, 128 devices: a whole 4x4x4 slice. The times are simulated.
128 devices in a mesh: hid: 16 (over x, y), wid: 4 (over z_lo, core), rep: 2 (over z_hi).
Axes of the slice: x: 4, y: 4, z: 4 (z_hi: 2, z_lo: 2; z = z_hi * 2 + z_lo), core: 2. Of those that a mesh axis runs over, the one named last changes fastest.
Arguments:
- grad_out: bfloat16 [2, 1024, 8192], P('rep', None, 'wid'), may hold values from -6 to 6
- down_weight: bfloat16 [28672, 8192], P('hid', 'wid'), may hold values from -0.03125 to 0.03125
- saved_gate: bfloat16 [2, 1024, 28672], P('rep', 'wid', 'hid'), may hold values from -6 to 6
- saved_up: bfloat16 [2, 1024, 28672], P('rep', 'wid', 'hid'), may hold values from -6 to 6
- saved_codes: int32 [2, 1024, 28672], P('rep', 'wid', 'hid'), may hold values from -128 to 127, as said below
- exponents: int32 [2, 1024, 224], P('rep', 'wid', 'hid'), may hold values from -12 to -9
Outputs:
- grad_gate: bfloat16 [2, 1024, 28672], P('rep', 'wid', 'hid')
- grad_up: bfloat16 [2, 1024, 28672], P('rep', 'wid', 'hid')
- grad_down: float32 [28672, 8192], P('hid', ('wid', 'rep'))
Inputs may be any that keep to these rules, and one draw needn't show every extreme that they name: `saved_codes`: codes at the clip limits -128 and 127 both occur.
All inputs are finite; a program needn't handle non-finite values.
Results may differ from a plain program's by a relative error of at most 0.014.
Values may be sent and summed in bfloat16 or wider, within the bound.
No kernel may reach another device: no remote copies, remote signals or barrier semaphores. Data moves between devices by JAX's collectives and lax.ppermute only.
A program may use at most 128 MiB of HBM per device.

v0:
```python
import math
import jax
import jax.numpy as jnp
from jax import lax
from jax.sharding import PartitionSpec as P

BLOCK = 128


def from_partner(block, axis, distance):
    count = lax.axis_size(axis)
    route = []
    for low in range(count):
        high = low | 1 << distance
        if high != low and high < count:
            route += [(low, high), (high, low)]
    return lax.ppermute(block, axis, route)


def sylvester(order):
    indices = jnp.arange(order, dtype=jnp.int32)
    both = jnp.bitwise_and(indices[:, None], indices[None, :])
    parity = jnp.zeros((order, order), jnp.int32)
    for bit_index in range(order.bit_length() - 1):
        parity = jnp.bitwise_xor(parity, jnp.bitwise_and(jnp.right_shift(both, bit_index), 1))
    return (1 - 2 * parity).astype(jnp.float32)


def block_transform(values, order):
    tok_local, hidden_local = values.shape
    table_block = sylvester(order) / math.sqrt(order)
    shaped = values.reshape(tok_local, hidden_local // order, order)
    shaped = jnp.einsum("tbk,kj->tbj", shaped, table_block, precision=lax.Precision.HIGHEST)
    return shaped.reshape(tok_local, hidden_local)


def shards(grad_out, down_weight, saved_gate, saved_up, saved_codes, exponents):
    out_rows = grad_out[0]
    codes_local = saved_codes[0]
    tok_local, hidden_local = codes_local.shape
    block_count = hidden_local // BLOCK
    scales = jnp.exp2(exponents[0].astype(jnp.float32))
    dequant = (
        (
            codes_local.astype(jnp.float32).reshape(tok_local, block_count, BLOCK)
            * scales[:, :, None]
        )
        .reshape(tok_local, hidden_local)
        .astype(jnp.bfloat16)
    )
    rows = out_rows
    grad_quant = lax.psum_scatter(
        lax.dot_general(
            rows, down_weight, (((1,), (1,)), ((), ())), preferred_element_type=jnp.float32
        ).astype(jnp.bfloat16),
        "wid",
        scatter_dimension=0,
        tiled=True,
    ).astype(jnp.float32)
    keep_mask = (codes_local > -128) & (codes_local < 127)
    masked = jnp.where(keep_mask, grad_quant, jnp.float32(0.0))
    mixed = block_transform(masked, BLOCK)
    group_count = lax.axis_size("hid")
    position = lax.axis_index("hid")
    for bit_index in range(group_count.bit_length() - 1):
        partner = from_partner(mixed.astype(jnp.bfloat16), "hid", bit_index).astype(mixed.dtype)
        upper = jnp.bitwise_and(jnp.right_shift(position, bit_index), 1) == 1
        mixed = jnp.where(upper, partner - mixed, mixed + partner)
    grad_hidden = mixed * (1.0 / math.sqrt(group_count))
    gate_local = saved_gate[0].astype(jnp.float32)
    up_local = saved_up[0].astype(jnp.float32)
    sigmoid_gate = jax.nn.sigmoid(gate_local)
    grad_gate = (
        grad_hidden * up_local * sigmoid_gate * (1.0 + gate_local * (1.0 - sigmoid_gate))
    ).astype(jnp.bfloat16)
    grad_up = (grad_hidden * gate_local * sigmoid_gate).astype(jnp.bfloat16)
    rows = out_rows
    replica_term = lax.dot_general(
        lax.all_gather(dequant, "wid", axis=0, tiled=True),
        rows,
        (((0,), (0,)), ((), ())),
        preferred_element_type=jnp.float32,
    )
    grad_down = lax.psum_scatter(
        replica_term.astype(jnp.bfloat16), "rep", scatter_dimension=1, tiled=True
    ).astype(jnp.float32)
    return (grad_gate[None], grad_up[None], grad_down)


def solution(mesh):
    in_specs = (
        P("rep", None, "wid"),
        P("hid", "wid"),
        P("rep", "wid", "hid"),
        P("rep", "wid", "hid"),
        P("rep", "wid", "hid"),
        P("rep", "wid", "hid"),
    )
    out_specs = (P("rep", "wid", "hid"), P("rep", "wid", "hid"), P("hid", ("wid", "rep")))
    return jax.shard_map(shards, mesh=mesh, in_specs=in_specs, out_specs=out_specs, check_vma=False)
```

profile of v0, /device:TPU:0, one launch (start us, length us, event | category | flops | bytes accessed | tf_op | source)
XLA Modules:
  0.0 223.2 jit_solution(2910662900731102619)
XLA Ops:
  7.2 0.0 copy-start.2
  7.2 0.0 all-gather.2.cloned.1.call-start
  7.2 1.8 copy.19
  9.0 0.0 copy-done.2
  9.1 1.1 fusion.20
  10.2 0.0 all-gather.2.cloned.1.call-update
  10.2 0.0 reduce-scatter.3.cloned.1.call-start
  10.3 13.0 %fusion.3 = bf16[1024,1792]{1,0:T(8,128)(2,1)} fusion(bf16[1792,2048]{1,0:T(8,128)(2,1)} %param.7, bf16[1,1024,2048]{2,1,0:T(8,128)(2,1)} %param.6), kind=kOutput, calls=%fused_computation.4 | convolution fusion | flops 7518027776 | bytes 15204352 | tf_op jit(solution)/shard_map/dot_general | solution.py:53
  23.2 0.0 reduce-scatter.3.cloned.1.call-update
  23.3 0.0 reduce-scatter.5.cloned.1.call-start
  23.3 31.0 %all-gather.2.cloned.1.call-done = bf16[1024,1792]{0,1:T(8,128)(2,1)} async-done(((bf16[256,1792]{0,1:T(8,128)(2,1)}), bf16[1024,1792]{0,1:T(8,128)(2,1)}) %all-gather.2.cloned.1.call-update) | async-done | bytes 3670032 | tf_op jit(solution)/shard_map/all_gather | solution.py:79
  54.4 12.5 %convolution_convert_fusion = bf16[1792,2048]{1,0:T(8,128)(2,1)} fusion(bf16[1024,1792]{0,1:T(8,128)(2,1)} %all-gather.2.cloned.1.call-done, bf16[1,1024,2048]{2,1,0:T(8,128)(2,1)} %param.6), kind=kOutput, calls=%fused_computation | convolution fusion | flops 7519862784 | bytes 15204352 | tf_op jit(solution)/shard_map/dot_general | solution.py:78
  66.9 0.0 reduce-scatter.5.cloned.1.call-update
  66.9 32.4 %reduce-scatter.3.cloned.1.call-done = bf16[256,1792]{1,0:T(8,128)(2,1)} async-done(((bf16[1024,1792]{1,0:T(8,128)(2,1)}), bf16[256,1792]{1,0:T(8,128)(2,1)}) %reduce-scatter.3.cloned.1.call-update) | async-done | bytes 917520 | tf_op jit(solution)/shard_map/reduce_scatter | solution.py:52
  99.3 2.7 %convert_select_fusion = f32[256,1792]{1,0:T(8,128)} fusion(bf16[256,1792]{1,0:T(8,128)(2,1)} %reduce-scatter.3.cloned.1.call-done, s32[1,256,1792]{2,1,0:T(8,128)S(1)} %copy-done.1), kind=kLoop, calls=%fused_computation.33 | loop fusion | flops 2293760 | bytes 4587520 | tf_op jit(solution)/shard_map/jit(_where)/select_n | solution.py:61
  102.1 1.8 copy.14
  103.9 3.1 %fusion.25 = f32[256,14,128]{0,2,1:T(8,128)} fusion(f32[256,14,128]{0,2,1:T(8,128)S(1)} %bitcast.43), kind=kOutput, calls=%fused_computation.38 | convolution fusion | flops 705052672 | bytes 3670016 | tf_op jit(solution)/shard_map/tbk,kj->tbj/dot_general | solution.py:33
  107.0 1.8 copy.16
  108.8 1.0 convert_element_type.79
  109.8 1.5 collective-permute-start
  111.3 21.2 %collective-permute-done = bf16[256,1792]{1,0:T(8,128)(2,1)S(1)} collective-permute-done((bf16[256,1792]{1,0:T(8,128)(2,1)}, bf16[256,1792]{1,0:T(8,128)(2,1)S(1)}, u32[]{:S(2)}, u32[]{:S(2)}) %collective-permute-start) | collective-permute-done | bytes 917536 | tf_op jit(solution)/shard_map/ppermute | solution.py:17
  132.4 1.2 fusion.22
  133.6 3.0 %collective-permute-start.1 = (bf16[256,1792]{1,0:T(8,128)(2,1)}, bf16[256,1792]{1,0:T(8,128)(2,1)}, u32[]{:S(2)}, u32[]{:S(2)}) collective-permute-start(bf16[256,1792]{1,0:T(8,128)(2,1)} %fusion.22), channel_id=1, source_target_pairs={{0,16},{16,0},{8,24},{24,8},{32,48},{48,32},{40,56},{56,40},{64,80... | collective-permute-start | bytes 2752520 | tf_op jit(solution)/shard_map/ppermute | solution.py:17
  136.6 20.5 %collective-permute-done.1 = bf16[256,1792]{1,0:T(8,128)(2,1)} collective-permute-done((bf16[256,1792]{1,0:T(8,128)(2,1)}, bf16[256,1792]{1,0:T(8,128)(2,1)}, u32[]{:S(2)}, u32[]{:S(2)}) %collective-permute-start.1) | collective-permute-done | bytes 917536 | tf_op jit(solution)/shard_map/ppermute | solution.py:17
  157.1 3.2 %fusion.70 = (bf16[256,1792]{1,0:T(8,128)(2,1)}, f32[256,1792]{1,0:T(8,128)}) fusion(f32[256,1792]{1,0:T(8,128)S(1)} %copy.16, bf16[256,1792]{1,0:T(8,128)(2,1)S(1)} %collective-permute-done, pred[]{:T(512)S(6)} %eq.15, bf16[256,1792]{1,0:T(8,128)(2,1)} %collective-permute-done.1, pred[]{:T(512)S(6)} %eq.14), kind=kLoop, calls=%fused_computation.85 | loop fusion | flops 4128768 | bytes 6422530 | tf_op jit(solution)/shard_map/convert_element_type | solution.py:66
  160.3 1.5 collective-permute-start.2
  161.8 19.7 %collective-permute-done.2 = bf16[256,1792]{1,0:T(8,128)(2,1)S(1)} collective-permute-done((bf16[256,1792]{1,0:T(8,128)(2,1)}, bf16[256,1792]{1,0:T(8,128)(2,1)S(1)}, u32[]{:S(2)}, u32[]{:S(2)}) %collective-permute-start.2) | collective-permute-done | bytes 917536 | tf_op jit(solution)/shard_map/ppermute | solution.py:17
  181.5 2.8 %fusion.21 = bf16[256,1792]{1,0:T(8,128)(2,1)} fusion(f32[256,1792]{1,0:T(8,128)} %get-tuple-element.4, bf16[256,1792]{1,0:T(8,128)(2,1)S(1)} %collective-permute-done.2, pred[]{:T(512)S(6)} %eq.13), kind=kLoop, calls=%fused_computation.34 | loop fusion | flops 2293760 | bytes 3670017 | tf_op jit(solution)/shard_map/convert_element_type | solution.py:66
  184.3 3.0 %collective-permute-start.3 = (bf16[256,1792]{1,0:T(8,128)(2,1)}, bf16[256,1792]{1,0:T(8,128)(2,1)}, u32[]{:S(2)}, u32[]{:S(2)}) collective-permute-start(bf16[256,1792]{1,0:T(8,128)(2,1)} %fusion.21), channel_id=1, source_target_pairs={{0,64},{64,0},{8,72},{72,8},{16,80},{80,16},{24,88},{88,24},{32,96... | collective-permute-start | bytes 2752520 | tf_op jit(solution)/shard_map/ppermute | solution.py:17
  187.3 19.0 %collective-permute-done.3 = bf16[256,1792]{1,0:T(8,128)(2,1)} collective-permute-done((bf16[256,1792]{1,0:T(8,128)(2,1)}, bf16[256,1792]{1,0:T(8,128)(2,1)}, u32[]{:S(2)}, u32[]{:S(2)}) %collective-permute-start.3) | collective-permute-done | bytes 917536 | tf_op jit(solution)/shard_map/ppermute | solution.py:17
  206.4 4.4 %fusion.23 = (bf16[1,256,1792]{2,1,0:T(8,128)(2,1)}, bf16[1,256,1792]{2,1,0:T(8,128)(2,1)}) fusion(bf16[1,256,1792]{2,1,0:T(8,128)(2,1)} %param.8, f32[256,1792]{1,0:T(8,128)S(1)} %copy-done, bf16[256,1792]{1,0:T(8,128)(2,1)S(1)} %collective-permute-done.2, pred[]{:T(512)S(6)} %eq.13, bf16[256,1792]{1,0:T(8,128)(2,1)} %collective-permute-done.3, ...), kind=kLoop, calls=%fused_computation.36 | loop fusion | flops 11010048 | bytes 7340034 | tf_op jit(solution)/shard_map/broadcast_in_dim | solution.py:87
  210.7 6.0 %convert_element_type.98 = f32[1792,1024]{1,0:T(8,128)} convert(bf16[1792,1024]{1,0:T(8,128)(2,1)} %reduce-scatter.5.cloned.1.call-done) | non-fusion elementwise | flops 1835008 | bytes 11010048 | tf_op jit(solution)/shard_map/convert_element_type | solution.py:86
  (7 shorter events, 0.0 us)
Async XLA Ops:
  7.2 1.9 copy-start.2
  7.2 47.2 %all-gather.2.cloned.1.call-start = ((), (), s32[]{:S(2)}) async-start(), calls=%async_computation.3 | async-start | bytes 4587520 | tf_op jit(solution)/shard_map/all_gather | solution.py:79
  10.2 89.1 %reduce-scatter.3.cloned.1.call-start = ((), (), s32[]{:S(2)}) async-start(), calls=%async_computation.2 | async-start | bytes 4587520 | tf_op jit(solution)/shard_map/reduce_scatter | solution.py:52
  23.3 187.5 %reduce-scatter.5.cloned.1.call-start = ((), (), s32[]{:S(2)}) async-start(), calls=%async_computation.4 | async-start | bytes 11010048 | tf_op jit(solution)/shard_map/reduce_scatter | solution.py:84
  66.9 32.5 %copy-start.1 = (s32[1,256,1792]{2,1,0:T(8,128)S(1)}, s32[1,256,1792]{2,1,0:T(8,128)}, u32[]{:S(2)}) copy-start(s32[1,256,1792]{2,1,0:T(8,128)} %param.10) | copy-start | bytes 5505028
  109.8 22.6 %collective-permute-start = (bf16[256,1792]{1,0:T(8,128)(2,1)}, bf16[256,1792]{1,0:T(8,128)(2,1)S(1)}, u32[]{:S(2)}, u32[]{:S(2)}) collective-permute-start(bf16[256,1792]{1,0:T(8,128)(2,1)} %convert_element_type.79), channel_id=1, source_target_pairs={{0,8},{8,0},{16,24},{24,16},{32,40},{40,32},{48,56},{56,48},{64,72... | collective-permute-start | bytes 2752520 | tf_op jit(solution)/shard_map/ppermute | solution.py:17
  133.6 23.5 %collective-permute-start.1 = (bf16[256,1792]{1,0:T(8,128)(2,1)}, bf16[256,1792]{1,0:T(8,128)(2,1)}, u32[]{:S(2)}, u32[]{:S(2)}) collective-permute-start(bf16[256,1792]{1,0:T(8,128)(2,1)} %fusion.22), channel_id=1, source_target_pairs={{0,16},{16,0},{8,24},{24,8},{32,48},{48,32},{40,56},{56,40},{64,80... | collective-permute-start | bytes 2752520 | tf_op jit(solution)/shard_map/ppermute | solution.py:17
  160.3 21.2 %collective-permute-start.2 = (bf16[256,1792]{1,0:T(8,128)(2,1)}, bf16[256,1792]{1,0:T(8,128)(2,1)S(1)}, u32[]{:S(2)}, u32[]{:S(2)}) collective-permute-start(bf16[256,1792]{1,0:T(8,128)(2,1)} %get-tuple-element.3), channel_id=1, source_target_pairs={{0,32},{32,0},{8,40},{40,8},{16,48},{48,16},{24,56},{56,24},{64,96... | collective-permute-start | bytes 2752520 | tf_op jit(solution)/shard_map/ppermute | solution.py:17
  181.5 24.8 %copy-start = (f32[256,1792]{1,0:T(8,128)S(1)}, f32[256,1792]{1,0:T(8,128)}, u32[]{:S(2)}) copy-start(f32[256,1792]{1,0:T(8,128)} %get-tuple-element.4) | copy-start | bytes 5505028
  184.3 22.0 %collective-permute-start.3 = (bf16[256,1792]{1,0:T(8,128)(2,1)}, bf16[256,1792]{1,0:T(8,128)(2,1)}, u32[]{:S(2)}, u32[]{:S(2)}) collective-permute-start(bf16[256,1792]{1,0:T(8,128)(2,1)} %fusion.21), channel_id=1, source_target_pairs={{0,64},{64,0},{8,72},{72,8},{16,80},{80,16},{24,88},{88,24},{32,96... | collective-permute-start | bytes 2752520 | tf_op jit(solution)/shard_map/ppermute | solution.py:17
Sparse Core Ops, SparseCore 0:
  10.3 43.9 all-gather.1
  56.8 42.5 reduce-scatter.2
  102.3 93.6 reduce-scatter.4
where the time goes:
time: 224 us; the launch traced here: 223 us
  waiting for transfers between devices  144 us (64%)
  matrix products  28.6 us (13%)
  other arithmetic  22.5 us (10%)
  between operations  13.8 us (6%)
  starting transfers between devices  9.1 us (4%)
  local copies, waits for them, and re-layouts  5.44 us (2%)
    ppermute x4, waiting for transfers between devices, from_partner(): return lax.ppermute(block, axis, route)  80.3 us
    reduce_scatter x1, waiting for transfers between devices, shards(): lax.psum_scatter(lax.dot_general(rows, down_weight, (((1,), (1,)), ((), (...  32.4 us
    all_gather x1, waiting for transfers between devices, shards(): lax.all_gather(dequant, 'wid', axis=0, tiled=True)  31 us
    dot_general x1, matrix products, shards(): lax.dot_general(rows, down_weight, (((1,), (1,)), ((), ())), preferred_el...  13 us
    dot_general x1, matrix products, shards(): lax.dot_general(lax.all_gather(dequant, 'wid', axis=0, tiled=True), rows,...  12.5 us
    ppermute x4, starting transfers between devices, from_partner(): return lax.ppermute(block, axis, route)  8.98 us
    convert_element_type x4, other arithmetic, shards(): mixed.astype(jnp.bfloat16)  8.26 us
    convert_element_type x1, other arithmetic, shards(): grad_down = lax.psum_scatter(replica_term.astype(jnp.bfloat16), 'rep', sc...  5.98 us
  transfers between devices with their start and end apart: 7, of which 6 were waited for; matrix products, arithmetic and copies ran while one was open for 21% of the time, Pallas kernels for 0%

commit v1 on v0

--- a/solution.py
+++ b/solution.py
@@ -76,7 +76,9 @@
     grad_up = (grad_hidden * gate_local * sigmoid_gate).astype(jnp.bfloat16)
     rows = out_rows
     replica_term = lax.dot_general(
-        lax.all_gather(dequant, "wid", axis=0, tiled=True),
+        jnp.concatenate(
+            lax.all_to_all(jnp.stack([dequant] * lax.axis_size("wid")), "wid", 0, 0), axis=0
+        ),
         rows,
         (((0,), (0,)), ((), ())),
         preferred_element_type=jnp.float32,

time: 224 us -> 236 us (1.054)
  blocking collectives: 0 us -> 74.3 us
  waiting for transfers between devices: 144 us -> 79 us
  local copies, waits for them, and re-layouts: 5.44 us -> 9.51 us
  matrix products: 28.6 us -> 26.2 us
    all_to_all x0 -> x1, blocking collectives: none -> 74.3 us  [shards(): lax.all_to_all(jnp.stack([dequant] * lax.axis_size('wid')), 'wid', 0, 0)]
    reduce_scatter x1, waiting for transfers between devices: 32.4 us -> 0.02 us  [shards(): lax.psum_scatter(lax.dot_general(rows, down_weight, (((1,), (1,)), ((), (...]
    all_gather x1 -> x0, waiting for transfers between devices: 31 us -> none  [shards(): lax.all_gather(dequant, 'wid', axis=0, tiled=True)]
    another operation x0 -> x2, local copies, waits for them, and re-layouts: none -> 2.79 us  [shards(): jnp.stack([dequant] * lax.axis_size('wid'))]
    dot_general x1, matrix products: 12.5 us -> 10.1 us  [shards(): lax.dot_general(jnp.concatenate(lax.all_to_all(jnp.stack([dequant] * lax....]
  transfers between devices with their start and end apart: 7 -> 6, of which waited for: 6 -> 4; matrix products, arithmetic and copies ran while one was open for 21% -> 16% of each run, Pallas kernels for 0% -> 0%
where the time goes in v1:
time: 236 us; the launch traced here: 235 us
  waiting for transfers between devices  79 us (33%)
  blocking collectives  74.3 us (31%)
  matrix products  26.2 us (11%)
  other arithmetic  23 us (10%)
  between operations  14.1 us (6%)
  local copies, waits for them, and re-layouts  9.51 us (4%)
  starting transfers between devices  9.04 us (4%)
    ppermute x4, waiting for transfers between devices, from_partner(): return lax.ppermute(block, axis, route)  79 us
    all_to_all x1, blocking collectives, shards(): lax.all_to_all(jnp.stack([dequant] * lax.axis_size('wid')), 'wid', 0, 0)  74.3 us
    dot_general x1, matrix products, shards(): lax.dot_general(rows, down_weight, (((1,), (1,)), ((), ())), preferred_el...  13 us
    dot_general x1, matrix products, shards(): lax.dot_general(jnp.concatenate(lax.all_to_all(jnp.stack([dequant] * lax....  10.1 us
    ppermute x4, starting transfers between devices, from_partner(): return lax.ppermute(block, axis, route)  8.96 us
    convert_element_type x4, other arithmetic, shards(): mixed.astype(jnp.bfloat16)  8.24 us
    convert_element_type x1, other arithmetic, shards(): grad_down = lax.psum_scatter(replica_term.astype(jnp.bfloat16), 'rep', sc...  5.98 us
  transfers between devices with their start and end apart: 6, of which 4 were waited for; matrix products, arithmetic and copies ran while one was open for 16% of the time, Pallas kernels for 0%

profile of v1, /device:TPU:0, one launch (start us, length us, event | category | flops | bytes accessed | tf_op | source)
XLA Modules:
  0.0 235.2 jit_solution(9088038018615069820)
XLA Ops:
  7.2 0.0 reduce-scatter.3.cloned.1.call-start
  7.2 13.0 %fusion.3 = bf16[1024,1792]{1,0:T(8,128)(2,1)} fusion(bf16[1792,2048]{1,0:T(8,128)(2,1)} %param.7, bf16[1,1024,2048]{2,1,0:T(8,128)(2,1)} %param.6), kind=kOutput, calls=%fused_computation.4 | convolution fusion | flops 7518027776 | bytes 15204352 | tf_op jit(solution)/shard_map/dot_general | solution.py:53
  20.2 0.0 reduce-scatter.3.cloned.1.call-update
  20.2 0.0 reduce-scatter.5.cloned.1.call-start
  20.3 1.4 copy-done.1
  21.7 1.7 copy.19
  23.4 1.7 fusion.20
  25.1 1.4 copy.20
  26.5 1.4 stack.10
  27.9 0.0 copy-start.3
  27.9 74.3 %all_to_all.5 = bf16[4,256,1792]{2,1,0:T(8,128)(2,1)S(1)} all-to-all(bf16[4,256,1792]{2,1,0:T(8,128)(2,1)S(1)} %stack.10), channel_id=1, replica_groups=mesh['hid'=16,'wid'=4,'rep'=2] {'wid'}, dimensions={0} | all-to-all | bytes 7340032 | tf_op jit(solution)/shard_map/all_to_all | solution.py:80
  102.2 10.1 %convolution_convert_fusion = bf16[1792,2048]{1,0:T(8,128)(2,1)} fusion(bf16[1024,1792]{1,0:T(8,128)(2,1)S(1)} %bitcast.45, bf16[1,1024,2048]{2,1,0:T(8,128)(2,1)S(1)} %copy-done.3), kind=kOutput, calls=%fused_computation | convolution fusion | flops 7519862784 | bytes 15204352 | tf_op jit(solution)/shard_map/dot_general | solution.py:78
  112.3 0.0 reduce-scatter.5.cloned.1.call-update
  112.3 0.0 reduce-scatter.3.cloned.1.call-done
  112.4 2.8 %convert_select_fusion = f32[256,1792]{1,0:T(8,128)} fusion(bf16[256,1792]{1,0:T(8,128)(2,1)} %reduce-scatter.3.cloned.1.call-done, s32[1,256,1792]{2,1,0:T(8,128)S(1)} %copy-done.1), kind=kLoop, calls=%fused_computation.33 | loop fusion | flops 2293760 | bytes 4587520 | tf_op jit(solution)/shard_map/jit(_where)/select_n | solution.py:61
  115.1 1.8 copy.14
  116.9 3.1 %fusion.25 = f32[256,14,128]{0,2,1:T(8,128)} fusion(f32[256,14,128]{0,2,1:T(8,128)S(1)} %bitcast.43), kind=kOutput, calls=%fused_computation.38 | convolution fusion | flops 705052672 | bytes 3670016 | tf_op jit(solution)/shard_map/tbk,kj->tbj/dot_general | solution.py:33
  120.0 1.8 copy.16
  121.9 1.0 convert_element_type.78
  122.9 1.5 collective-permute-start
  124.4 20.9 %collective-permute-done = bf16[256,1792]{1,0:T(8,128)(2,1)S(1)} collective-permute-done((bf16[256,1792]{1,0:T(8,128)(2,1)}, bf16[256,1792]{1,0:T(8,128)(2,1)S(1)}, u32[]{:S(2)}, u32[]{:S(2)}) %collective-permute-start) | collective-permute-done | bytes 917536 | tf_op jit(solution)/shard_map/ppermute | solution.py:17
  145.2 1.2 fusion.22
  146.4 3.0 %collective-permute-start.1 = (bf16[256,1792]{1,0:T(8,128)(2,1)}, bf16[256,1792]{1,0:T(8,128)(2,1)}, u32[]{:S(2)}, u32[]{:S(2)}) collective-permute-start(bf16[256,1792]{1,0:T(8,128)(2,1)} %fusion.22), channel_id=1, source_target_pairs={{0,16},{16,0},{8,24},{24,8},{32,48},{48,32},{40,56},{56,40},{64,80... | collective-permute-start | bytes 2752520 | tf_op jit(solution)/shard_map/ppermute | solution.py:17
  149.5 20.2 %collective-permute-done.1 = bf16[256,1792]{1,0:T(8,128)(2,1)} collective-permute-done((bf16[256,1792]{1,0:T(8,128)(2,1)}, bf16[256,1792]{1,0:T(8,128)(2,1)}, u32[]{:S(2)}, u32[]{:S(2)}) %collective-permute-start.1) | collective-permute-done | bytes 917536 | tf_op jit(solution)/shard_map/ppermute | solution.py:17
  169.6 3.2 %fusion.70 = (bf16[256,1792]{1,0:T(8,128)(2,1)}, f32[256,1792]{1,0:T(8,128)}) fusion(f32[256,1792]{1,0:T(8,128)S(1)} %copy.16, bf16[256,1792]{1,0:T(8,128)(2,1)S(1)} %collective-permute-done, pred[]{:T(512)S(6)} %eq.15, bf16[256,1792]{1,0:T(8,128)(2,1)} %collective-permute-done.1, pred[]{:T(512)S(6)} %eq.14), kind=kLoop, calls=%fused_computation.85 | loop fusion | flops 4128768 | bytes 6422530 | tf_op jit(solution)/shard_map/convert_element_type | solution.py:66
  172.8 1.5 collective-permute-start.2
  174.3 19.3 %collective-permute-done.2 = bf16[256,1792]{1,0:T(8,128)(2,1)S(1)} collective-permute-done((bf16[256,1792]{1,0:T(8,128)(2,1)}, bf16[256,1792]{1,0:T(8,128)(2,1)S(1)}, u32[]{:S(2)}, u32[]{:S(2)}) %collective-permute-start.2) | collective-permute-done | bytes 917536 | tf_op jit(solution)/shard_map/ppermute | solution.py:17
  193.6 2.8 %fusion.21 = bf16[256,1792]{1,0:T(8,128)(2,1)} fusion(f32[256,1792]{1,0:T(8,128)} %get-tuple-element.4, bf16[256,1792]{1,0:T(8,128)(2,1)S(1)} %collective-permute-done.2, pred[]{:T(512)S(6)} %eq.13), kind=kLoop, calls=%fused_computation.34 | loop fusion | flops 2293760 | bytes 3670017 | tf_op jit(solution)/shard_map/convert_element_type | solution.py:66
  196.4 3.0 %collective-permute-start.3 = (bf16[256,1792]{1,0:T(8,128)(2,1)}, bf16[256,1792]{1,0:T(8,128)(2,1)}, u32[]{:S(2)}, u32[]{:S(2)}) collective-permute-start(bf16[256,1792]{1,0:T(8,128)(2,1)} %fusion.21), channel_id=1, source_target_pairs={{0,64},{64,0},{8,72},{72,8},{16,80},{80,16},{24,88},{88,24},{32,96... | collective-permute-start | bytes 2752520 | tf_op jit(solution)/shard_map/ppermute | solution.py:17
  199.4 18.6 %collective-permute-done.3 = bf16[256,1792]{1,0:T(8,128)(2,1)} collective-permute-done((bf16[256,1792]{1,0:T(8,128)(2,1)}, bf16[256,1792]{1,0:T(8,128)(2,1)}, u32[]{:S(2)}, u32[]{:S(2)}) %collective-permute-start.3) | collective-permute-done | bytes 917536 | tf_op jit(solution)/shard_map/ppermute | solution.py:17
  218.0 4.4 %fusion.23 = (bf16[1,256,1792]{2,1,0:T(8,128)(2,1)}, bf16[1,256,1792]{2,1,0:T(8,128)(2,1)}) fusion(bf16[1,256,1792]{2,1,0:T(8,128)(2,1)} %param.8, f32[256,1792]{1,0:T(8,128)S(1)} %copy-done, bf16[256,1792]{1,0:T(8,128)(2,1)S(1)} %collective-permute-done.2, pred[]{:T(512)S(6)} %eq.13, bf16[256,1792]{1,0:T(8,128)(2,1)} %collective-permute-done.3, ...), kind=kLoop, calls=%fused_computation.36 | loop fusion | flops 11010048 | bytes 7340034 | tf_op jit(solution)/shard_map/broadcast_in_dim | solution.py:89
  222.4 6.0 %convert_element_type.96 = f32[1792,1024]{1,0:T(8,128)} convert(bf16[1792,1024]{1,0:T(8,128)(2,1)} %reduce-scatter.5.cloned.1.call-done) | non-fusion elementwise | flops 1835008 | bytes 11010048 | tf_op jit(solution)/shard_map/convert_element_type | solution.py:88
  (9 shorter events, 0.0 us)
Async XLA Ops:
  7.2 105.2 %reduce-scatter.3.cloned.1.call-start = ((), (), s32[]{:S(2)}) async-start(), calls=%async_computation.3 | async-start | bytes 4587520 | tf_op jit(solution)/shard_map/reduce_scatter | solution.py:52
  20.2 1.5 copy-start.1
  20.2 3.2 %copy-start.2 = (s32[1,256,14]{1,0,2:T(1,128)S(1)}, s32[1,256,14]{1,0,2:T(1,128)}, u32[]{:S(2)}) copy-start(s32[1,256,14]{1,0,2:T(1,128)} %param.11) | copy-start | bytes 43012
  20.2 202.2 %reduce-scatter.5.cloned.1.call-start = ((), (), s32[]{:S(2)}) async-start(), calls=%async_computation.4 | async-start | bytes 11010048 | tf_op jit(solution)/shard_map/reduce_scatter | solution.py:86
  27.9 74.3 %copy-start.3 = (bf16[1,1024,2048]{2,1,0:T(8,128)(2,1)S(1)}, bf16[1,1024,2048]{2,1,0:T(8,128)(2,1)}, u32[]{:S(2)}) copy-start(bf16[1,1024,2048]{2,1,0:T(8,128)(2,1)} %param.6) | copy-start | bytes 12582916
  122.9 22.4 %collective-permute-start = (bf16[256,1792]{1,0:T(8,128)(2,1)}, bf16[256,1792]{1,0:T(8,128)(2,1)S(1)}, u32[]{:S(2)}, u32[]{:S(2)}) collective-permute-start(bf16[256,1792]{1,0:T(8,128)(2,1)} %convert_element_type.78), channel_id=1, source_target_pairs={{0,8},{8,0},{16,24},{24,16},{32,40},{40,32},{48,56},{56,48},{64,72... | collective-permute-start | bytes 2752520 | tf_op jit(solution)/shard_map/ppermute | solution.py:17
  146.4 23.2 %collective-permute-start.1 = (bf16[256,1792]{1,0:T(8,128)(2,1)}, bf16[256,1792]{1,0:T(8,128)(2,1)}, u32[]{:S(2)}, u32[]{:S(2)}) collective-permute-start(bf16[256,1792]{1,0:T(8,128)(2,1)} %fusion.22), channel_id=1, source_target_pairs={{0,16},{16,0},{8,24},{24,8},{32,48},{48,32},{40,56},{56,40},{64,80... | collective-permute-start | bytes 2752520 | tf_op jit(solution)/shard_map/ppermute | solution.py:17
  172.8 20.8 %collective-permute-start.2 = (bf16[256,1792]{1,0:T(8,128)(2,1)}, bf16[256,1792]{1,0:T(8,128)(2,1)S(1)}, u32[]{:S(2)}, u32[]{:S(2)}) collective-permute-start(bf16[256,1792]{1,0:T(8,128)(2,1)} %get-tuple-element.3), channel_id=1, source_target_pairs={{0,32},{32,0},{8,40},{40,8},{16,48},{48,16},{24,56},{56,24},{64,96... | collective-permute-start | bytes 2752520 | tf_op jit(solution)/shard_map/ppermute | solution.py:17
  193.6 24.4 %copy-start = (f32[256,1792]{1,0:T(8,128)S(1)}, f32[256,1792]{1,0:T(8,128)}, u32[]{:S(2)}) copy-start(f32[256,1792]{1,0:T(8,128)} %get-tuple-element.4) | copy-start | bytes 5505028
  196.4 21.6 %collective-permute-start.3 = (bf16[256,1792]{1,0:T(8,128)(2,1)}, bf16[256,1792]{1,0:T(8,128)(2,1)}, u32[]{:S(2)}, u32[]{:S(2)}) collective-permute-start(bf16[256,1792]{1,0:T(8,128)(2,1)} %fusion.21), channel_id=1, source_target_pairs={{0,64},{64,0},{8,72},{72,8},{16,80},{80,16},{24,88},{88,24},{32,96... | collective-permute-start | bytes 2752520 | tf_op jit(solution)/shard_map/ppermute | solution.py:17
Sparse Core Ops, SparseCore 0:
  20.3 71.4 reduce-scatter.2
  112.5 93.6 reduce-scatter.4
